TPU v7x, 32 devices: a whole 2x2x4 slice. The times are simulated.
32 devices in a mesh: freq: 4 (over z), space: 8 (over y, x, core).
Axes of the slice: x: 2, y: 2, z: 4, core: 2. Of those that a mesh axis runs over, the one named last changes fastest.
Arguments:
- recorded: bfloat16 [8, 2, 2048, 128], P('freq', None, 'space'), may hold values from -6 to 6
- v_factors: bfloat16 [8, 8, 2, 2048, 128], P('freq', None, None, 'space'), may hold values from -0.25 to 0.25
- u_factors: bfloat16 [8, 2, 2048, 8, 128], P('freq', None, 'space'), may hold values from -0.25 to 0.25
- tile_ranks: int32 [8, 8, 8], P('freq'), may hold values from 0 to 128, as said below
- mute_start: int32 [2048, 128], P('space', 'freq'), may hold values from 0 to 127
Outputs:
- muted_traces: float32 [2048, 128, 128], P('space', 'freq')
Inputs may be any that keep to these rules, and one draw needn't show every extreme that they name: `tile_ranks`: entries with i equal to j are 128; every other entry is 0 or 64.
All inputs are finite; a program needn't handle non-finite values.
Results may differ from a plain program's by a relative error of at most 0.0041.
Values may be sent and summed in bfloat16 or wider, within the bound.
A program may use at most 64 MiB of HBM per device.

v0:
```python
import functools
import math

import jax
import jax.numpy as jnp
import ml_dtypes
import numpy as np
from jax import lax
from jax.experimental import pallas as pl
from jax.experimental.pallas import tpu as pltpu
from jax.sharding import PartitionSpec as P

NT = 128
GROUP = 8
NT_DIMS = (((1,), (1,)), ((), ()))


def flipped(index, mask):
    result = index
    bit = 1
    while bit <= mask:
        if mask & bit:
            result = result + bit * (1 - 2 * ((index // bit) % 2))
        bit *= 2
    return result


def send_order(count):
    return sorted(range(count), key=lambda r: (-bin(r >> 1).count("1"), r % 2, r))


def spectra_kernel(
    tiles, parts, ranks_hbm, recorded_hbm, v_hbm, u_hbm, mute_hbm, out_hbm, mask_hbm,
    ranks_ref, recorded_ref, mute_ref, mask_ref, v_ref, u_ref, wide_ref, data_ref, send_ref, recv_ref, own_ref, factor_ref, spec_ref,
    v_sems, u_sems, send_sems, recv_sems, zsend_sems, zrecv_sems,
    keep_sems, first_sems, mask_sems,
):
    me = lax.axis_index("space")
    me_z = lax.axis_index("freq")
    freqs = recorded_ref.shape[0]
    tile = recorded_ref.shape[2]
    sources = recorded_ref.shape[3]
    ranks = v_ref.shape[3]
    half = ranks // 2
    share = sources // parts
    order = send_order(tiles)

    v_copies = [
        pltpu.make_async_copy(v_hbm.at[f], v_ref.at[f], v_sems.at[f]) for f in range(freqs)
    ]
    u_copies = [
        pltpu.make_async_copy(u_hbm.at[f], u_ref.at[f], u_sems.at[f]) for f in range(freqs)
    ]
    ranks_copy = pltpu.make_async_copy(ranks_hbm, ranks_ref, first_sems.at[0])
    data_copy = pltpu.make_async_copy(recorded_hbm, recorded_ref, first_sems.at[1])
    mute_copy = pltpu.make_async_copy(mute_hbm, mute_ref, first_sems.at[2])
    data_copy.start()
    ranks_copy.start()
    for copy in v_copies + u_copies:
        copy.start()
    mute_copy.start()

    barrier = pltpu.get_barrier_semaphore()
    for r in range(1, tiles):
        pl.semaphore_signal(
            barrier, inc=1, device_id={"space": flipped(me, r)}, device_id_type=pl.DeviceIdType.MESH
        )
    for r in range(1, parts):
        pl.semaphore_signal(
            barrier, inc=1, device_id={"freq": flipped(me_z, r)},
            device_id_type=pl.DeviceIdType.MESH,
        )

    def space_copy(f, r):
        return pltpu.make_async_remote_copy(
            src_ref=send_ref.at[f, r],
            dst_ref=recv_ref.at[f, me],
            send_sem=send_sems.at[f, r],
            recv_sem=recv_sems.at[f, r],
            device_id={"space": flipped(me, r)},
            device_id_type=pl.DeviceIdType.MESH,
        )

    rows = tile // parts

    def freq_copy(f, c, r):
        target = flipped(me_z, r)
        return pltpu.make_async_remote_copy(
            src_ref=spec_ref.at[f, target, pl.ds(c * rows, rows)],
            dst_ref=out_hbm.at[me_z, f, pl.ds(c * rows, rows)],
            send_sem=zsend_sems.at[f, c, r],
            recv_sem=zrecv_sems.at[f, c, r],
            device_id={"freq": target},
            device_id_type=pl.DeviceIdType.MESH,
        )

    def keep_copy(f, c):
        return pltpu.make_async_copy(
            spec_ref.at[f, me_z, pl.ds(c * rows, rows)],
            out_hbm.at[me_z, f, pl.ds(c * rows, rows)],
            keep_sems.at[f, c],
        )

    data_copy.wait()
    lane = lax.broadcasted_iota(jnp.int32, (sources, ranks), 1)
    low = lane < half
    rank_of = lax.rem(lane, half)
    ranks_copy.wait()
    for f in range(freqs):
        real = recorded_ref[f, 0].astype(jnp.float32).T.astype(jnp.bfloat16)
        imag = recorded_ref[f, 1].astype(jnp.float32).T.astype(jnp.bfloat16)
        data_ref[f, :sources, :tile] = real
        data_ref[f, :sources, tile:] = -imag
        data_ref[f, sources:, :tile] = imag
        data_ref[f, sources:, tile:] = real
        v_copies[f].wait()
        for first in range(0, tiles, 4):
            group = order[first : first + 4]
            targets = [flipped(me, r) for r in group]
            packed_v = jnp.concatenate([v_ref[f, row, :, :half] for row in targets], axis=1)
            blocks = jnp.dot(data_ref[f], packed_v, preferred_element_type=jnp.float32)
            for n, (r, row) in enumerate(zip(group, targets)):
                columns = slice((n // 2) * ranks, (n // 2 + 1) * ranks)
                real, imag = blocks[:sources, columns], blocks[sources:, columns]
                if n % 2 == 0:
                    packed = jnp.where(low, real, pltpu.roll(imag, half, 1))
                else:
                    packed = jnp.where(low, pltpu.roll(real, half, 1), imag)
                packed = jnp.where(rank_of < ranks_ref[f, row, me], packed, 0.0).astype(jnp.bfloat16)
                if r == 0:
                    recv_ref[f, me] = packed
                else:
                    send_ref[f, r] = packed
                    if f == 0 and r == order[0]:
                        pl.semaphore_wait(barrier, tiles - 1 + parts - 1)
                    space_copy(f, r).start()
    for f in range(freqs):
        blocks = jnp.dot(data_ref[f], v_ref[f, me], preferred_element_type=jnp.float32)
        packed = jnp.where(low, pltpu.roll(blocks[:sources], half, 1), blocks[sources:])
        kept = rank_of + half < ranks_ref[f, me, me]
        own_ref[f] = jnp.where(kept, packed, 0.0).astype(jnp.bfloat16)

    wide_lane = lax.broadcasted_iota(jnp.int32, (tile, ranks), 1)
    wide_low = wide_lane < half
    def prepare(f):
        u_copies[f].wait()
        for c in range(2):
            wide_ref[c] = u_ref[f, c].astype(jnp.float32)
        for j in range(tiles + 1):
            start = j if j < tiles else me
            real = wide_ref[0, pl.ds(start, tile, stride=tiles), :]
            imag = wide_ref[1, pl.ds(start, tile, stride=tiles), :]
            real_roll = pltpu.roll(real, half, 1)
            imag_roll = pltpu.roll(imag, half, 1)
            if j < tiles:
                top = jnp.where(wide_low, real, -imag_roll)
                bottom = jnp.where(wide_low, imag, real_roll)
            else:
                top = jnp.where(wide_low, real_roll, -imag)
                bottom = jnp.where(wide_low, imag_roll, real)
            factor_ref[f, j, :tile] = top.astype(jnp.bfloat16)
            factor_ref[f, j, tile:] = bottom.astype(jnp.bfloat16)

    swap_lane = lax.broadcasted_iota(jnp.int32, (rows, sources), 1)
    for f in range(freqs):
        prepare(f)
        total = lax.dot_general(
            factor_ref[f, tiles], own_ref[f], NT_DIMS, preferred_element_type=jnp.float32
        )
        for first in [0] + list(range(2, tiles, 2))[::-1]:
            pair = [flipped(me, first), flipped(me, first + 1)]
            for r in (first, first + 1):
                if r > 0:
                    space_copy(f, r).wait_recv()
            lhs = jnp.concatenate([factor_ref[f, j] for j in pair], axis=1)
            rhs = jnp.concatenate([recv_ref[f, j] for j in pair], axis=1)
            total += lax.dot_general(lhs, rhs, NT_DIMS, preferred_element_type=jnp.float32)
        for c in range(2):
            pieces = [total[c * tile + q * rows : c * tile + (q + 1) * rows] for q in range(parts)]
            bit = parts // 2
            while bit >= 1:
                width = bit * share
                keep = lax.rem(swap_lane, 2 * width) < width
                swapped = list(pieces)
                for q in range(parts):
                    if not q & bit:
                        x, y = pieces[q], pieces[q + bit]
                        swapped[q] = jnp.where(keep, x, pltpu.roll(y, width, 1))
                        swapped[q + bit] = jnp.where(keep, pltpu.roll(x, sources - width, 1), y)
                pieces = swapped
                bit //= 2
            for z in range(parts):
                spec_ref[f, z, c * rows : (c + 1) * rows] = pieces[z].astype(jnp.bfloat16)
            for r in range(parts - 1, 0, -1):
                freq_copy(f, c, r).start()
            keep_copy(f, c).start()

    mute_copy.wait()
    times = lax.broadcasted_iota(jnp.int32, (share, NT), 1)
    span = 2 * GROUP
    mask_copies = []
    for n in range(rows // span):
        for q in range(parts):
            for i in range(span):
                p = q * rows + n * span + i
                at = (q * span + i) * share
                starts = mute_ref[:, p : p + 1]
                mask_ref[n, at : at + share] = jnp.where(times >= starts, 1.0, 0.0).astype(jnp.bfloat16)
        copy = pltpu.make_async_copy(mask_ref.at[n], mask_hbm.at[n], mask_sems.at[n])
        copy.start()
        mask_copies.append(copy)

    for copy in mask_copies:
        copy.wait()
    for f in range(freqs):
        for r in range(1, tiles):
            space_copy(f, r).wait_send()
        for c in range(2):
            keep_copy(f, c).wait()
            for r in range(1, parts):
                freq_copy(f, c, r).wait_send()
                freq_copy(f, c, r).wait_recv()


def time_kernel(
    share, spec_hbm, mask_hbm, basis_hbm, out_hbm,
    spec_ref, mask_ref, basis_ref, rows_ref, in_sems, mask_sems, out_sems,
):
    parts, freqs, rows, sources = spec_ref.shape
    rows //= 2
    spec_copy = pltpu.make_async_copy(spec_hbm, spec_ref, in_sems.at[0])
    spec_copy.start()
    basis_copy = pltpu.make_async_copy(basis_hbm, basis_ref, in_sems.at[1])
    basis_copy.start()
    mask_copies = [
        pltpu.make_async_copy(mask_hbm.at[n], mask_ref.at[n], mask_sems.at[n])
        for n in range(mask_ref.shape[0])
    ]
    for copy in mask_copies:
        copy.start()
    spec_copy.wait()
    copies = []
    for n in range(rows // (2 * GROUP)):
        sides = []
        for g in (2 * n, 2 * n + 1):
            pieces = []
            for z in range(parts):
                for f in range(freqs):
                    for c in range(2):
                        at = c * rows + g * GROUP
                        pieces.append(spec_ref[z, f, at : at + GROUP].astype(jnp.float32))
            block = jnp.concatenate(pieces, axis=0)
            sides.append(block.T.astype(jnp.bfloat16))
        lhs = jnp.concatenate(sides, axis=0)
        lhs = jnp.concatenate([lhs, lhs], axis=1)
        if n == 0:
            basis_copy.wait()
        mask_copies[n].wait()
        for pair in range(GROUP // 2):
            product = jnp.dot(
                lhs, basis_ref[:, pair * 2 * NT : (pair + 1) * 2 * NT], preferred_element_type=jnp.float32
            )
            for side in range(2):
                for q in range(parts):
                    for e in range(2):
                        p = q * rows + (2 * n + side) * GROUP + pair * 2 + e
                        at = side * sources + q * share
                        values = product[at : at + share, e * NT : (e + 1) * NT]
                        row = (q * 2 * GROUP + side * GROUP + pair * 2 + e) * share
                        mask = mask_ref[n, row : row + share].astype(jnp.float32)
                        rows_ref[p * share : (p + 1) * share, :] = values * mask
        for q in range(parts):
            span = pl.ds((q * rows + 2 * n * GROUP) * share, 2 * GROUP * share)
            copy = pltpu.make_async_copy(rows_ref.at[span], out_hbm.at[span], out_sems.at[n, q])
            copy.start()
            copies.append(copy)
    for copy in copies:
        copy.wait()


def block_basis(freq_total):
    weights = 1 + np.arange(freq_total) * (NT // 2 // freq_total)
    phase = (weights[:, None] * np.arange(NT)[None, :] % NT) * (2.0 * math.pi / NT)
    scale = 1.0 / math.sqrt(2.0 * freq_total)
    table = np.stack([np.cos(phase) * scale, -np.sin(phase) * scale], axis=1)
    table = table.reshape(2 * freq_total, NT).astype(np.float32)
    high = table.astype(ml_dtypes.bfloat16)
    low = (table - high.astype(np.float32)).astype(ml_dtypes.bfloat16)
    both = np.stack([high, low])
    full = np.zeros((2, 2 * freq_total, GROUP, GROUP, NT), ml_dtypes.bfloat16)
    for g in range(GROUP):
        full[:, :, g, g, :] = both
    return full.reshape(4 * freq_total * GROUP, GROUP * NT)


def shards(tiles, parts, basis, recorded, v_factors, u_factors, tile_ranks, mute_start):
    freqs, _, tile, sources = recorded.shape
    ranks = v_factors.shape[4]
    share = sources // parts
    bf16 = jnp.bfloat16
    spec_shape = (parts, freqs, 2 * tile // parts, sources)
    chunks = tile // parts // (2 * GROUP)
    mask_shape = (chunks, tile * share // chunks, NT)
    anywhere = pl.BlockSpec(memory_space=pl.ANY)
    spectra, mask = pl.pallas_call(
        functools.partial(spectra_kernel, tiles, parts),
        out_shape=(jax.ShapeDtypeStruct(spec_shape, bf16), jax.ShapeDtypeStruct(mask_shape, bf16)),
        in_specs=[anywhere] * 5,
        out_specs=(anywhere, anywhere),
        scratch_shapes=[
            pltpu.SMEM(tile_ranks.shape, jnp.int32),
            pltpu.VMEM(recorded.shape, bf16),
            pltpu.VMEM((share, tile), jnp.int32),
            pltpu.VMEM(mask_shape, bf16),
            pltpu.VMEM((freqs, tiles, 2 * tile, ranks), bf16),
            pltpu.VMEM((freqs, 2, tile * tiles, ranks), bf16),
            pltpu.VMEM((2, tile * tiles, ranks), jnp.float32),
            pltpu.VMEM((freqs, 2 * sources, 2 * tile), bf16),
            pltpu.VMEM((freqs, tiles, sources, ranks), bf16),
            pltpu.VMEM((freqs, tiles, sources, ranks), bf16),
            pltpu.VMEM((freqs, sources, ranks), bf16),
            pltpu.VMEM((freqs, tiles + 1, 2 * tile, ranks), bf16),
            pltpu.VMEM((freqs, parts, 2 * tile // parts, sources), bf16),
            pltpu.SemaphoreType.DMA((freqs,)),
            pltpu.SemaphoreType.DMA((freqs,)),
            pltpu.SemaphoreType.DMA((freqs, tiles)),
            pltpu.SemaphoreType.DMA((freqs, tiles)),
            pltpu.SemaphoreType.DMA((freqs, 2, parts)),
            pltpu.SemaphoreType.DMA((freqs, 2, parts)),
            pltpu.SemaphoreType.DMA((freqs, 2)),
            pltpu.SemaphoreType.DMA((3,)),
            pltpu.SemaphoreType.DMA((chunks,)),
        ],
        compiler_params=pltpu.CompilerParams(collective_id=0, has_side_effects=True),
        name="spectra_kernel",
    )(
        tile_ranks,
        recorded,
        v_factors.reshape(freqs, tiles, 2 * tile, ranks),
        u_factors.reshape(freqs, 2, tile * tiles, ranks),
        mute_start.T,
    )
    traces = pl.pallas_call(
        functools.partial(time_kernel, share),
        out_shape=jax.ShapeDtypeStruct((tile * share, NT), jnp.float32),
        in_specs=[anywhere] * 3,
        out_specs=anywhere,
        scratch_shapes=[
            pltpu.VMEM(spec_shape, bf16),
            pltpu.VMEM(mask_shape, bf16),
            pltpu.VMEM(basis.shape, bf16),
            pltpu.VMEM((tile * share, NT), jnp.float32),
            pltpu.SemaphoreType.DMA((2,)),
            pltpu.SemaphoreType.DMA((chunks,)),
            pltpu.SemaphoreType.DMA((chunks, parts)),
        ],
        name="time_kernel",
    )(spectra, mask, jnp.asarray(basis))
    return traces.reshape(tile, share, NT)


def solution(mesh):
    placed = (
        P("freq", None, "space", None),
        P("freq", None, None, "space", None),
        P("freq", None, "space", None, None),
        P("freq", None, None),
        P("space", "freq"),
    )
    tiles, parts = mesh.shape["space"], mesh.shape["freq"]

    def run(*args):
        body = functools.partial(shards, tiles, parts, block_basis(args[0].shape[0]))
        return jax.shard_map(
            body, mesh=mesh, in_specs=placed, out_specs=P("space", "freq", None), check_vma=False
        )(*args)

    return run
```

profile of v0, /device:TPU:0, one launch (start us, length us, event | category | flops | bytes accessed | tf_op | source)
XLA Modules:
  0.0 23.7 jit_solution(4706877015651739836)
XLA Ops:
  0.0 19.6 %spectra_kernel.1 = (bf16[4,2,128,128]{3,2,1,0:T(8,128)(2,1)}, bf16[4,2048,128]{2,1,0:T(8,128)(2,1)}) custom-call(s32[2,8,8]{2,1,0:T(8,128)} %ranks_hbm.1, bf16[2,2,256,128]{3,2,1,0:T(8,128)(2,1)} %recorded_hbm.1, bf16[2,8,512,128]{3,2,1,0:T(8,128)(2,1)} %bitcast.4, bf16[2,2,2048,128]{3,2,1,0:T(8,128)(2,1)} %bitcast.5, s32[32,256]{1,0:T(8,128)} %bitcast.6), custom_call_target="tpu_custom_call" | custom-call | tf_op jit(solution)/shard_map/spectra_kernel/pallas_call | solution.py:305
  19.6 4.1 %time_kernel.1 = f32[8192,128]{1,0:T(8,128)} custom-call(bf16[4,2,128,128]{3,2,1,0:T(8,128)(2,1)} %get-tuple-element.7.spec_hbm, bf16[4,2048,128]{2,1,0:T(8,128)(2,1)} %get-tuple-element.8.mask_hbm, bf16[256,1024]{1,0:T(8,128)(2,1)} %constant.2.clone.basis_hbm), custom_call_target="tpu_custom_call" | custom-call | tf_op jit(solution)/shard_map/time_kernel/pallas_call | solution.py:343
where the time goes:
time: 23.8 us; the launch traced here: 23.7 us
  Pallas kernels  23.7 us (100%)
    pallas_call x1, Pallas kernels, shards(): pl.pallas_call(functools.partial(spectra_kernel, tiles, parts), out_shape...  19.6 us
    pallas_call x1, Pallas kernels, shards(): pl.pallas_call(functools.partial(time_kernel, share), out_shape=jax.Shape...  4.09 us

commit v1 on v0

v1 whole, which is shorter than its diff:
```python
import functools
import math

import jax
import jax.numpy as jnp
import ml_dtypes
import numpy as np
from jax import lax
from jax.experimental import pallas as pl
from jax.experimental.pallas import tpu as pltpu
from jax.sharding import PartitionSpec as P

NT = 128
GROUP = 8
NT_DIMS = (((1,), (1,)), ((), ()))


def flipped(index, mask):
    result = index
    bit = 1
    while bit <= mask:
        if mask & bit:
            result = result + bit * (1 - 2 * ((index // bit) % 2))
        bit *= 2
    return result


def nth_target(step, me_z, parts):
    if step == parts - 1:
        return me_z
    return step + (step - me_z + parts) // parts


def spectra_kernel(
    tiles, parts, ranks_hbm, recorded_hbm, v_hbm, u_hbm, mute_hbm, out_ref, mask_ref,
    ranks_ref, recorded_ref, mute_ref, v_ref, u_ref, wide_ref, data_ref, send_ref, recv_ref, factor_ref, spec_ref,
    v_sems, u_sems, send_sems, recv_sems, zsend_sems, zrecv_sems, first_sems,
):
    me = lax.axis_index("space")
    me_z = lax.axis_index("freq")
    freqs = recorded_ref.shape[0]
    tile = recorded_ref.shape[2]
    sources = recorded_ref.shape[3]
    ranks = v_ref.shape[3]
    half = ranks // 2
    share = sources // parts
    rows = tile // parts
    order = list(range(tiles - 1, -1, -1))

    v_copies = [
        pltpu.make_async_copy(v_hbm.at[f], v_ref.at[f], v_sems.at[f]) for f in range(freqs)
    ]
    u_copies = [
        pltpu.make_async_copy(u_hbm.at[f], u_ref.at[f], u_sems.at[f]) for f in range(freqs)
    ]
    ranks_copy = pltpu.make_async_copy(ranks_hbm, ranks_ref, first_sems.at[0])
    data_copy = pltpu.make_async_copy(recorded_hbm, recorded_ref, first_sems.at[1])
    mute_copy = pltpu.make_async_copy(mute_hbm, mute_ref, first_sems.at[2])
    data_copy.start()
    ranks_copy.start()
    for copy in v_copies + u_copies:
        copy.start()
    mute_copy.start()

    barrier = pltpu.get_barrier_semaphore()
    for r in range(1, tiles):
        pl.semaphore_signal(
            barrier, inc=1, device_id={"space": flipped(me, r)}, device_id_type=pl.DeviceIdType.MESH
        )
    for r in range(1, parts):
        pl.semaphore_signal(
            barrier, inc=1, device_id={"freq": flipped(me_z, r)},
            device_id_type=pl.DeviceIdType.MESH,
        )

    def space_copy(f, n, r):
        return pltpu.make_async_remote_copy(
            src_ref=send_ref.at[f, n, r],
            dst_ref=recv_ref.at[f, n, r],
            send_sem=send_sems.at[f, n],
            recv_sem=recv_sems.at[f, n],
            device_id={"space": flipped(me, r)},
            device_id_type=pl.DeviceIdType.MESH,
        )

    def arrivals(ref, sem):
        return pltpu.make_async_copy(ref.at[pl.ds(1, tiles - 1)], ref.at[pl.ds(1, tiles - 1)], sem)

    def send_step(f, n):
        for r in order[:-1]:
            space_copy(f, n, r).start()

    def freq_copy(f, n):
        return pltpu.make_async_remote_copy(
            src_ref=spec_ref.at[f, n],
            dst_ref=out_ref.at[me_z, f],
            send_sem=zsend_sems.at[f, n],
            recv_sem=zrecv_sems.at[f, me_z],
            device_id={"freq": nth_target(n, me_z, parts)},
            device_id_type=pl.DeviceIdType.MESH,
        )

    lane = lax.broadcasted_iota(jnp.int32, (share, ranks), 1)
    low = lane < half
    rank_of = lax.rem(lane, half)
    data_copy.wait()
    for f in range(freqs):
        real = recorded_ref[f, 0].astype(jnp.float32).T.astype(jnp.bfloat16)
        imag = recorded_ref[f, 1].astype(jnp.float32).T.astype(jnp.bfloat16)
        for z in range(parts):
            part = slice(z * share, (z + 1) * share)
            data_ref[f, z, :share, :tile] = real[part]
            data_ref[f, z, :share, tile:] = -imag[part]
            data_ref[f, z, share:, :tile] = -imag[part]
            data_ref[f, z, share:, tile:] = -real[part]
    ranks_copy.wait()

    def first_stage(f):
        v_copies[f].wait()
        lhs = jnp.concatenate([data_ref[f, nth_target(n, me_z, parts)] for n in range(parts)], axis=0)
        for first in range(0, tiles, 2):
            group = order[first : first + 2]
            targets = [flipped(me, r) for r in group]
            pair = jnp.concatenate([v_ref[f, row] for row in targets], axis=1)
            blocks = jnp.dot(lhs, pair, preferred_element_type=jnp.float32)
            for t, (r, row) in enumerate(zip(group, targets)):
                columns = slice(t * ranks, (t + 1) * ranks)
                limit = ranks_ref[f, row, me]
                keep = rank_of < limit
                for n in range(parts):
                    at = n * 2 * share
                    real, imag = blocks[at : at + share, columns], blocks[at + share : at + 2 * share, columns]
                    packed = jnp.where(low, real, pltpu.roll(imag, half, 1))
                    packed = jnp.where(keep, packed, 0.0).astype(jnp.bfloat16)
                    if r == 0:
                        recv_ref[f, n, 0] = packed
                        packed = jnp.where(low, pltpu.roll(real, half, 1), imag)
                        kept = rank_of + half < limit
                        recv_ref[f, n, tiles] = jnp.where(kept, packed, 0.0).astype(jnp.bfloat16)
                    else:
                        send_ref[f, n, r] = packed

    for f in range(freqs):
        first_stage(f)
        if f == 0:
            pl.semaphore_wait(barrier, tiles - 1 + parts - 1)
        send_step(f, 0)
    for n in range(1, parts):
        for f in range(freqs):
            send_step(f, n)

    wide_low = lax.broadcasted_iota(jnp.int32, (tile, ranks), 1) < half

    def prepare(f):
        u_copies[f].wait()
        for c in range(2):
            wide_ref[c] = u_ref[f, c].astype(jnp.float32)
        for r in range(tiles):
            start = flipped(me, r)
            real = wide_ref[0, pl.ds(start, tile, stride=tiles), :]
            imag = wide_ref[1, pl.ds(start, tile, stride=tiles), :]
            packed = jnp.where(wide_low, real, pltpu.roll(imag, half, 1))
            factor_ref[f, :, r * ranks : (r + 1) * ranks] = packed.astype(jnp.bfloat16)
            if r == 0:
                packed = jnp.where(wide_low, pltpu.roll(real, half, 1), imag)
                factor_ref[f, :, tiles * ranks :] = packed.astype(jnp.bfloat16)

    for f in range(freqs):
        prepare(f)

    swap_lane = lax.broadcasted_iota(jnp.int32, (rows, sources), 1)
    for n in range(parts):
        for f in range(freqs):
            arrivals(recv_ref.at[f, n], recv_sems.at[f, n]).wait()
            plain, turned = [], []
            for r in range(tiles + 1):
                block = recv_ref[f, n, r]
                plain.append(block)
                swapped = pltpu.roll(block.astype(jnp.float32), half, 1)
                turned.append(jnp.where(low, -swapped, swapped).astype(jnp.bfloat16))
            rhs = jnp.concatenate(
                [jnp.concatenate(plain, axis=1), jnp.concatenate(turned, axis=1)], axis=0
            )
            total = lax.dot_general(factor_ref[f], rhs, NT_DIMS, preferred_element_type=jnp.float32)
            if total.shape[1] < sources:
                total = jnp.concatenate([total, total], axis=1)
            for c in range(2):
                merged = None
                for q in range(parts):
                    piece = total[q * rows : (q + 1) * rows]
                    shift = (q - c) * share % sources
                    if shift:
                        piece = pltpu.roll(piece, shift, 1)
                    merged = piece if q == 0 else jnp.where(swap_lane < q * share, merged, piece)
                merged = merged.astype(jnp.bfloat16)
                if n == parts - 1:
                    out_ref[me_z, f, c * rows : (c + 1) * rows] = merged
                else:
                    spec_ref[f, n, c * rows : (c + 1) * rows] = merged
            if n < parts - 1:
                freq_copy(f, n).start()

    mute_copy.wait()
    times = lax.broadcasted_iota(jnp.int32, (share, NT), 1)
    span = 2 * GROUP
    for n in range(rows // span):
      for q in range(parts):
          for i in range(span):
              p = q * rows + n * span + i
              at = (q * span + i) * share
              starts = mute_ref[:, p : p + 1]
              mask_ref[n, at : at + share] = jnp.where(times >= starts, 1.0, 0.0).astype(jnp.bfloat16)

    for n in range(parts):
        for f in range(freqs):
            arrivals(send_ref.at[f, n], send_sems.at[f, n]).wait()
    for n in range(parts - 1):
        for f in range(freqs):
            freq_copy(f, n).wait_send()
    for r in range(1, parts):
        for f in range(freqs):
            source = flipped(me_z, r)
            pltpu.make_async_copy(
                out_ref.at[source, f], out_ref.at[source, f], zrecv_sems.at[f, source]
            ).wait()


def time_kernel(
    share, spec_ref, mask_ref, basis_ref, out_hbm, rows_ref, out_sems,
):
    parts, freqs, rows, sources = spec_ref.shape
    rows //= 2
    copies = []
    for n in range(rows // (2 * GROUP)):
        sides = []
        for g in (2 * n, 2 * n + 1):
            pieces = []
            for z in range(parts):
                for f in range(freqs):
                    for c in range(2):
                        at = c * rows + g * GROUP
                        pieces.append(spec_ref[z, f, at : at + GROUP].astype(jnp.float32))
            block = jnp.concatenate(pieces, axis=0)
            sides.append(block.T.astype(jnp.bfloat16))
        lhs = jnp.concatenate(sides, axis=0)
        lhs = jnp.concatenate([lhs, lhs], axis=1)
        for pair in range(GROUP // 2):
            product = jnp.dot(
                lhs, basis_ref[:, pair * 2 * NT : (pair + 1) * 2 * NT], preferred_element_type=jnp.float32
            )
            for side in range(2):
                for q in range(parts):
                    for e in range(2):
                        p = q * rows + (2 * n + side) * GROUP + pair * 2 + e
                        at = side * sources + q * share
                        values = product[at : at + share, e * NT : (e + 1) * NT]
                        row = (q * 2 * GROUP + side * GROUP + pair * 2 + e) * share
                        mask = mask_ref[n, row : row + share].astype(jnp.float32)
                        rows_ref[p * share : (p + 1) * share, :] = values * mask
        for q in range(parts):
            span = pl.ds((q * rows + 2 * n * GROUP) * share, 2 * GROUP * share)
            copy = pltpu.make_async_copy(rows_ref.at[span], out_hbm.at[span], out_sems.at[n, q])
            copy.start()
            copies.append(copy)
    for copy in copies:
        copy.wait()


def block_basis(freq_total):
    weights = 1 + np.arange(freq_total) * (NT // 2 // freq_total)
    phase = (weights[:, None] * np.arange(NT)[None, :] % NT) * (2.0 * math.pi / NT)
    scale = 1.0 / math.sqrt(2.0 * freq_total)
    table = np.stack([np.cos(phase) * scale, -np.sin(phase) * scale], axis=1)
    table = table.reshape(2 * freq_total, NT).astype(np.float32)
    high = table.astype(ml_dtypes.bfloat16)
    low = (table - high.astype(np.float32)).astype(ml_dtypes.bfloat16)
    both = np.stack([high, low])
    full = np.zeros((2, 2 * freq_total, GROUP, GROUP, NT), ml_dtypes.bfloat16)
    for g in range(GROUP):
        full[:, :, g, g, :] = both
    return full.reshape(4 * freq_total * GROUP, GROUP * NT)


def shards(tiles, parts, basis, recorded, v_factors, u_factors, tile_ranks, mute_start):
    freqs, _, tile, sources = recorded.shape
    ranks = v_factors.shape[4]
    share = sources // parts
    bf16 = jnp.bfloat16
    spec_shape = (parts, freqs, 2 * tile // parts, sources)
    chunks = tile // parts // (2 * GROUP)
    mask_shape = (chunks, tile * share // chunks, NT)
    anywhere = pl.BlockSpec(memory_space=pl.ANY)
    spectra, mask = pl.pallas_call(
        functools.partial(spectra_kernel, tiles, parts),
        out_shape=(pltpu.VMEM(spec_shape, bf16), pltpu.VMEM(mask_shape, bf16)),
        in_specs=[pl.BlockSpec(memory_space=pltpu.HBM)] * 5,
        out_specs=(pl.BlockSpec(memory_space=pltpu.VMEM),)*2,
        scratch_shapes=[
            pltpu.SMEM(tile_ranks.shape, jnp.int32),
            pltpu.VMEM(recorded.shape, bf16),
            pltpu.VMEM((share, tile), jnp.int32),
            pltpu.VMEM((freqs, tiles, 2 * tile, ranks), bf16),
            pltpu.VMEM((freqs, 2, tile * tiles, ranks), bf16),
            pltpu.VMEM((2, tile * tiles, ranks), jnp.float32),
            pltpu.VMEM((freqs, parts, 2 * share, 2 * tile), bf16),
            pltpu.VMEM((freqs, parts, tiles, share, ranks), bf16),
            pltpu.VMEM((freqs, parts, tiles + 1, share, ranks), bf16),
            pltpu.VMEM((freqs, tile, (tiles + 1) * ranks), bf16),
            pltpu.VMEM((freqs, parts - 1, 2 * tile // parts, sources), bf16),
            pltpu.SemaphoreType.DMA((freqs,)),
            pltpu.SemaphoreType.DMA((freqs,)),
            pltpu.SemaphoreType.DMA((freqs, parts)),
            pltpu.SemaphoreType.DMA((freqs, parts)),
            pltpu.SemaphoreType.DMA((freqs, parts - 1)),
            pltpu.SemaphoreType.DMA((freqs, parts)),
            pltpu.SemaphoreType.DMA((3,)),
        ],
        compiler_params=pltpu.CompilerParams(collective_id=0, has_side_effects=True, vmem_limit_bytes=48 << 20),
        name="spectra_kernel",
    )(
        *[pltpu.with_memory_space_constraint(x, pltpu.HBM) for x in (tile_ranks,
        recorded,
        v_factors.reshape(freqs, tiles, 2 * tile, ranks),
        u_factors.reshape(freqs, 2, tile * tiles, ranks),
        mute_start.T)],
    )
    traces = pl.pallas_call(
        functools.partial(time_kernel, share),
        out_shape=jax.ShapeDtypeStruct((tile * share, NT), jnp.float32),
        in_specs=[pl.BlockSpec(memory_space=pltpu.VMEM)]*3,
        out_specs=pl.BlockSpec(memory_space=pltpu.HBM),
        compiler_params=pltpu.CompilerParams(vmem_limit_bytes=48 << 20),
        scratch_shapes=[
            pltpu.VMEM((tile * share, NT), jnp.float32),
            pltpu.SemaphoreType.DMA((chunks, parts)),
        ],
        name="time_kernel",
    )(spectra, mask, jnp.asarray(basis))
    return traces.reshape(tile, share, NT)


def solution(mesh):
    placed = (
        P("freq", None, "space", None),
        P("freq", None, None, "space", None),
        P("freq", None, "space", None, None),
        P("freq", None, None),
        P("space", "freq"),
    )
    tiles, parts = mesh.shape["space"], mesh.shape["freq"]

    def run(*args):
        body = functools.partial(shards, tiles, parts, block_basis(args[0].shape[0]))
        return jax.shard_map(
            body, mesh=mesh, in_specs=placed, out_specs=P("space", "freq", None), check_vma=False
        )(*args)

    return run
```

time: 23.8 us -> 19.6 us (0.82)
  Pallas kernels: 23.7 us -> 19.4 us
    pallas_call x1, Pallas kernels: 19.6 us -> 16.9 us  [shards(): pl.pallas_call(functools.partial(spectra_kernel, tiles, parts), out_shape...]
    pallas_call x1, Pallas kernels: 4.09 us -> 2.48 us  [shards(): pl.pallas_call(functools.partial(time_kernel, share), out_shape=jax.Shape...]
where the time goes in v1:
time: 19.6 us; the launch traced here: 19.4 us
  Pallas kernels  19.4 us (99%)
    pallas_call x1, Pallas kernels, shards(): pl.pallas_call(functools.partial(spectra_kernel, tiles, parts), out_shape...  16.9 us
    pallas_call x1, Pallas kernels, shards(): pl.pallas_call(functools.partial(time_kernel, share), out_shape=jax.Shape...  2.48 us

profile of v1, /device:TPU:0, one launch (start us, length us, event | category | flops | bytes accessed | tf_op | source)
XLA Modules:
  0.0 19.4 jit_solution(987015958506465167)
XLA Ops:
  0.0 0.0 copy-start
  0.0 16.9 %spectra_kernel.1 = (bf16[4,2,128,128]{3,2,1,0:T(8,128)(2,1)S(1)}, bf16[4,2048,128]{2,1,0:T(8,128)(2,1)S(1)}) custom-call(s32[2,8,8]{2,1,0:T(8,128)} %ranks_hbm.1, bf16[2,2,256,128]{3,2,1,0:T(8,128)(2,1)} %recorded_hbm.1, bf16[2,8,512,128]{3,2,1,0:T(8,128)(2,1)} %bitcast.4, bf16[2,2,2048,128]{3,2,1,0:T(8,128)(2,1)} %bitcast.5, s32[32,256]{1,0:T(8,128)} %bitcast.6), custom_call_target="tpu_custom_call" | custom-call | tf_op jit(solution)/shard_map/spectra_kernel/pallas_call | solution.py:293
  16.9 0.0 copy-done
  16.9 2.5 %time_kernel.1 = f32[8192,128]{1,0:T(8,128)} custom-call(bf16[4,2,128,128]{3,2,1,0:T(8,128)(2,1)S(1)} %get-tuple-element.7.spec_ref, bf16[4,2048,128]{2,1,0:T(8,128)(2,1)S(1)} %get-tuple-element.8.mask_ref, bf16[256,1024]{1,0:T(8,128)(2,1)S(1)} %copy-done), custom_call_target="tpu_custom_call" | custom-call | tf_op jit(solution)/shard_map/time_kernel/pallas_call | solution.py:327
Async XLA Ops:
  0.0 16.9 %copy-start = (bf16[256,1024]{1,0:T(8,128)(2,1)S(1)}, bf16[256,1024]{1,0:T(8,128)(2,1)}, u32[]{:S(2)}) copy-start(bf16[256,1024]{1,0:T(8,128)(2,1)} %constant.2.clone.basis_ref) | copy-start | bytes 1572868

commit v2 on v1

--- a/solution.py
+++ b/solution.py
@@ -12,6 +12,7 @@
 
 NT = 128
 GROUP = 8
+LIMIT = 8
 NT_DIMS = (((1,), (1,)), ((), ()))
 
 
@@ -25,16 +26,35 @@
     return result
 
 
-def nth_target(step, me_z, parts):
-    if step == parts - 1:
-        return me_z
-    return step + (step - me_z + parts) // parts
+def crossed(index, other, count):
+    result = 0
+    bit = 1
+    while bit < count:
+        here, there = index // bit % 2, other // bit % 2
+        result = result + bit * (here + there - 2 * here * there)
+        bit *= 2
+    return result
+
+
+def visit_order(parts):
+    rows = [list(range(parts - 1, -1, -1))]
+    for z in range(1, parts):
+        others = [x for x in range(1, parts) if x != z]
+        rows.append([0] + sorted(others, key=lambda x: (abs(x - z), x)) + [z])
+    return rows
+
+
+def chosen(rows, index):
+    count = len(rows)
+    reached = [(index - z + count) // count for z in range(count)] + [0]
+    here = [reached[z] - reached[z + 1] for z in range(count)]
+    return [sum(rows[z][n] * here[z] for z in range(count)) for n in range(count)]
 
 
 def spectra_kernel(
     tiles, parts, ranks_hbm, recorded_hbm, v_hbm, u_hbm, mute_hbm, out_ref, mask_ref,
     ranks_ref, recorded_ref, mute_ref, v_ref, u_ref, wide_ref, data_ref, send_ref, recv_ref, factor_ref, spec_ref,
-    v_sems, u_sems, send_sems, recv_sems, zsend_sems, zrecv_sems, first_sems,
+    v_sems, u_sems, send_sems, recv_sems, first_sems, ready_sem,
 ):
     me = lax.axis_index("space")
     me_z = lax.axis_index("freq")
@@ -46,6 +66,8 @@
     share = sources // parts
     rows = tile // parts
     order = list(range(tiles - 1, -1, -1))
+    visits = chosen(visit_order(parts), me_z)
+    small = tiles <= LIMIT
 
     v_copies = [
         pltpu.make_async_copy(v_hbm.at[f], v_ref.at[f], v_sems.at[f]) for f in range(freqs)
@@ -53,12 +75,13 @@
     u_copies = [
         pltpu.make_async_copy(u_hbm.at[f], u_ref.at[f], u_sems.at[f]) for f in range(freqs)
     ]
-    ranks_copy = pltpu.make_async_copy(ranks_hbm, ranks_ref, first_sems.at[0])
-    data_copy = pltpu.make_async_copy(recorded_hbm, recorded_ref, first_sems.at[1])
+    data_copy = pltpu.make_async_copy(recorded_hbm, recorded_ref, first_sems.at[0])
+    ranks_copy = pltpu.make_async_copy(ranks_hbm, ranks_ref, first_sems.at[1])
     mute_copy = pltpu.make_async_copy(mute_hbm, mute_ref, first_sems.at[2])
     data_copy.start()
+    v_copies[0].start()
     ranks_copy.start()
-    for copy in v_copies + u_copies:
+    for copy in v_copies[1:] + u_copies:
         copy.start()
     mute_copy.start()
 
@@ -68,35 +91,34 @@
             barrier, inc=1, device_id={"space": flipped(me, r)}, device_id_type=pl.DeviceIdType.MESH
         )
     for r in range(1, parts):
-        pl.semaphore_signal(
-            barrier, inc=1, device_id={"freq": flipped(me_z, r)},
-            device_id_type=pl.DeviceIdType.MESH,
-        )
+        peer = flipped(me_z, r)
+
+        @pl.when(peer > me_z)
+        def _(peer=peer):
+            pl.semaphore_signal(
+                barrier, inc=1, device_id={"freq": peer}, device_id_type=pl.DeviceIdType.MESH
+            )
 
     def space_copy(f, n, r):
         return pltpu.make_async_remote_copy(
             src_ref=send_ref.at[f, n, r],
             dst_ref=recv_ref.at[f, n, r],
-            send_sem=send_sems.at[f, n],
+            send_sem=send_sems.at[0],
             recv_sem=recv_sems.at[f, n],
-            device_id={"space": flipped(me, r)},
+            device_id={"space": flipped(me, r) if small else crossed(me, r, tiles)},
             device_id_type=pl.DeviceIdType.MESH,
         )
 
     def arrivals(ref, sem):
         return pltpu.make_async_copy(ref.at[pl.ds(1, tiles - 1)], ref.at[pl.ds(1, tiles - 1)], sem)
-
-    def send_step(f, n):
-        for r in order[:-1]:
-            space_copy(f, n, r).start()
 
     def freq_copy(f, n):
         return pltpu.make_async_remote_copy(
             src_ref=spec_ref.at[f, n],
             dst_ref=out_ref.at[me_z, f],
-            send_sem=zsend_sems.at[f, n],
-            recv_sem=zrecv_sems.at[f, me_z],
-            device_id={"freq": nth_target(n, me_z, parts)},
+            send_sem=send_sems.at[1],
+            recv_sem=send_sems.at[2],
+            device_id={"freq": visits[n]},
             device_id_type=pl.DeviceIdType.MESH,
         )
 
@@ -115,9 +137,15 @@
             data_ref[f, z, share:, tile:] = -real[part]
     ranks_copy.wait()
 
-    def first_stage(f):
-        v_copies[f].wait()
-        lhs = jnp.concatenate([data_ref[f, nth_target(n, me_z, parts)] for n in range(parts)], axis=0)
+    def send_all(f, steps, low_end, high_end):
+        def body(i, _):
+            for n in steps:
+                space_copy(f, n, i).start()
+
+        lax.fori_loop(low_end, high_end, body, None)
+
+    def first_stage(f, steps):
+        lhs = jnp.concatenate([data_ref[f, visits[n]] for n in steps], axis=0)
         for first in range(0, tiles, 2):
             group = order[first : first + 2]
             targets = [flipped(me, r) for r in group]
@@ -127,8 +155,8 @@
                 columns = slice(t * ranks, (t + 1) * ranks)
                 limit = ranks_ref[f, row, me]
                 keep = rank_of < limit
-                for n in range(parts):
-                    at = n * 2 * share
+                for i, n in enumerate(steps):
+                    at = i * 2 * share
                     real, imag = blocks[at : at + share, columns], blocks[at + share : at + 2 * share, columns]
                     packed = jnp.where(low, real, pltpu.roll(imag, half, 1))
                     packed = jnp.where(keep, packed, 0.0).astype(jnp.bfloat16)
@@ -139,16 +167,41 @@
                         recv_ref[f, n, tiles] = jnp.where(kept, packed, 0.0).astype(jnp.bfloat16)
                     else:
                         send_ref[f, n, r] = packed
+            done = first + 2
+            if not small and done % LIMIT == 0:
+                send_all(f, steps, max(tiles - done, 1), tiles - done + LIMIT)
+
+    def send_step(f, n):
+        if small:
+            for r in order[:-1]:
+                space_copy(f, n, r).start()
+
+    def enter():
+        pl.semaphore_wait(barrier, tiles - 1 + me_z)
+        for r in range(1, parts):
+            peer = flipped(me_z, r)
+
+            @pl.when(peer < me_z)
+            def _(peer=peer):
+                pl.semaphore_signal(
+                    ready_sem, inc=1, device_id={"freq": peer}, device_id_type=pl.DeviceIdType.MESH
+                )
+
+    if not small:
+        enter()
 
     for f in range(freqs):
-        first_stage(f)
-        if f == 0:
-            pl.semaphore_wait(barrier, tiles - 1 + parts - 1)
+        v_copies[f].wait()
+        first_stage(f, [0])
+        if f == 0 and small:
+            enter()
         send_step(f, 0)
-    for n in range(1, parts):
+    for f in range(freqs):
+        first_stage(f, range(1, parts))
+        send_step(f, 1)
+    for n in range(2, parts):
         for f in range(freqs):
             send_step(f, n)
-
     wide_low = lax.broadcasted_iota(jnp.int32, (tile, ranks), 1) < half
 
     def prepare(f):
@@ -168,6 +221,25 @@
     for f in range(freqs):
         prepare(f)
 
+    mute_copy.wait()
+    times = lax.broadcasted_iota(jnp.int32, (share, NT), 1).astype(jnp.float32).astype(jnp.bfloat16)
+    one = jnp.ones((share, NT), jnp.bfloat16)
+    zero = jnp.zeros((share, NT), jnp.bfloat16)
+    span = 2 * GROUP
+
+    def make_masks():
+        begins = mute_ref[...].astype(jnp.float32).astype(jnp.bfloat16)
+        for n in range(rows // span):
+            for q in range(parts):
+                for i in range(span):
+                    p = q * rows + n * span + i
+                    at = (q * span + i) * share
+                    mask_ref[n, at : at + share] = jnp.where(times >= begins[:, p : p + 1], one, zero)
+
+    @pl.when(me_z == 0)
+    def _():
+        make_masks()
+
     swap_lane = lax.broadcasted_iota(jnp.int32, (rows, sources), 1)
     for n in range(parts):
         for f in range(freqs):
@@ -181,7 +253,13 @@
             rhs = jnp.concatenate(
                 [jnp.concatenate(plain, axis=1), jnp.concatenate(turned, axis=1)], axis=0
             )
-            total = lax.dot_general(factor_ref[f], rhs, NT_DIMS, preferred_element_type=jnp.float32)
+            total = jnp.concatenate(
+                [
+                    lax.dot_general(factor_ref[f, at : at + tile // 2], rhs, NT_DIMS, preferred_element_type=jnp.float32)
+                    for at in (0, tile // 2)
+                ],
+                axis=0,
+            )
             if total.shape[1] < sources:
                 total = jnp.concatenate([total, total], axis=1)
             for c in range(2):
@@ -197,40 +275,32 @@
                     out_ref[me_z, f, c * rows : (c + 1) * rows] = merged
                 else:
                     spec_ref[f, n, c * rows : (c + 1) * rows] = merged
+            if n == 0 and f == 0:
+                @pl.when(me_z < parts - 1)
+                def _():
+                    pl.semaphore_wait(ready_sem, parts - 1 - me_z)
+
             if n < parts - 1:
                 freq_copy(f, n).start()
 
-    mute_copy.wait()
-    times = lax.broadcasted_iota(jnp.int32, (share, NT), 1)
-    span = 2 * GROUP
-    for n in range(rows // span):
-      for q in range(parts):
-          for i in range(span):
-              p = q * rows + n * span + i
-              at = (q * span + i) * share
-              starts = mute_ref[:, p : p + 1]
-              mask_ref[n, at : at + share] = jnp.where(times >= starts, 1.0, 0.0).astype(jnp.bfloat16)
-
-    for n in range(parts):
-        for f in range(freqs):
-            arrivals(send_ref.at[f, n], send_sems.at[f, n]).wait()
-    for n in range(parts - 1):
-        for f in range(freqs):
-            freq_copy(f, n).wait_send()
-    for r in range(1, parts):
-        for f in range(freqs):
-            source = flipped(me_z, r)
-            pltpu.make_async_copy(
-                out_ref.at[source, f], out_ref.at[source, f], zrecv_sems.at[f, source]
-            ).wait()
+
+    @pl.when(me_z > 0)
+    def _():
+        make_masks()
+
+    everything = send_ref.at[:, :, pl.ds(1, tiles - 1)]
+    pltpu.make_async_copy(everything, everything, send_sems.at[0]).wait()
+    foreign = spec_ref
+    pltpu.make_async_copy(foreign, foreign, send_sems.at[1]).wait()
+    foreign = out_ref.at[pl.ds(0, parts - 1)]
+    pltpu.make_async_copy(foreign, foreign, send_sems.at[2]).wait()
 
 
 def time_kernel(
-    share, spec_ref, mask_ref, basis_ref, out_hbm, rows_ref, out_sems,
+    share, spec_ref, mask_ref, basis_ref, out_hbm, rows_ref, out_sem,
 ):
     parts, freqs, rows, sources = spec_ref.shape
     rows //= 2
-    copies = []
     for n in range(rows // (2 * GROUP)):
         sides = []
         for g in (2 * n, 2 * n + 1):
@@ -259,11 +329,9 @@
                         rows_ref[p * share : (p + 1) * share, :] = values * mask
         for q in range(parts):
             span = pl.ds((q * rows + 2 * n * GROUP) * share, 2 * GROUP * share)
-            copy = pltpu.make_async_copy(rows_ref.at[span], out_hbm.at[span], out_sems.at[n, q])
+            copy = pltpu.make_async_copy(rows_ref.at[span], out_hbm.at[span], out_sem)
             copy.start()
-            copies.append(copy)
-    for copy in copies:
-        copy.wait()
+    pltpu.make_async_copy(rows_ref, out_hbm, out_sem).wait()
 
 
 def block_basis(freq_total):
@@ -309,11 +377,10 @@
             pltpu.VMEM((freqs, parts - 1, 2 * tile // parts, sources), bf16),
             pltpu.SemaphoreType.DMA((freqs,)),
             pltpu.SemaphoreType.DMA((freqs,)),
-            pltpu.SemaphoreType.DMA((freqs, parts)),
-            pltpu.SemaphoreType.DMA((freqs, parts)),
-            pltpu.SemaphoreType.DMA((freqs, parts - 1)),
+            pltpu.SemaphoreType.DMA((3,)),
             pltpu.SemaphoreType.DMA((freqs, parts)),
             pltpu.SemaphoreType.DMA((3,)),
+            pltpu.SemaphoreType.REGULAR,
         ],
         compiler_params=pltpu.CompilerParams(collective_id=0, has_side_effects=True, vmem_limit_bytes=48 << 20),
         name="spectra_kernel",
@@ -332,7 +399,7 @@
         compiler_params=pltpu.CompilerParams(vmem_limit_bytes=48 << 20),
         scratch_shapes=[
             pltpu.VMEM((tile * share, NT), jnp.float32),
-            pltpu.SemaphoreType.DMA((chunks, parts)),
+            pltpu.SemaphoreType.DMA,
         ],
         name="time_kernel",
     )(spectra, mask, jnp.asarray(basis))

time: 19.6 us -> 17.6 us (0.90)
  Pallas kernels: 19.4 us -> 17.5 us
    pallas_call x1, Pallas kernels: 16.9 us -> 15.1 us  [shards(): pl.pallas_call(functools.partial(spectra_kernel, tiles, parts), out_shape...]
where the time goes in v2:
time: 17.6 us; the launch traced here: 17.5 us
  Pallas kernels  17.5 us (99%)
    pallas_call x1, Pallas kernels, shards(): pl.pallas_call(functools.partial(spectra_kernel, tiles, parts), out_shape...  15.1 us
    pallas_call x1, Pallas kernels, shards(): pl.pallas_call(functools.partial(time_kernel, share), out_shape=jax.Shape...  2.35 us

profile of v2, /device:TPU:0, one launch (start us, length us, event | category | flops | bytes accessed | tf_op | source)
XLA Modules:
  0.0 17.5 jit_solution(4905020916043610603)
XLA Ops:
  0.0 0.0 copy-start
  0.0 15.1 %spectra_kernel.1 = (bf16[4,2,128,128]{3,2,1,0:T(8,128)(2,1)S(1)}, bf16[4,2048,128]{2,1,0:T(8,128)(2,1)S(1)}) custom-call(s32[2,8,8]{2,1,0:T(8,128)} %ranks_hbm.1, bf16[2,2,256,128]{3,2,1,0:T(8,128)(2,1)} %recorded_hbm.1, bf16[2,8,512,128]{3,2,1,0:T(8,128)(2,1)} %bitcast.4, bf16[2,2,2048,128]{3,2,1,0:T(8,128)(2,1)} %bitcast.5, s32[32,256]{1,0:T(8,128)} %bitcast.6), custom_call_target="tpu_custom_call" | custom-call | tf_op jit(solution)/shard_map/spectra_kernel/pallas_call | solution.py:361
  15.1 0.0 copy-done
  15.1 2.3 %time_kernel.1 = f32[8192,128]{1,0:T(8,128)} custom-call(bf16[4,2,128,128]{3,2,1,0:T(8,128)(2,1)S(1)} %get-tuple-element.7.spec_ref, bf16[4,2048,128]{2,1,0:T(8,128)(2,1)S(1)} %get-tuple-element.8.mask_ref, bf16[256,1024]{1,0:T(8,128)(2,1)S(1)} %copy-done), custom_call_target="tpu_custom_call" | custom-call | tf_op jit(solution)/shard_map/time_kernel/pallas_call | solution.py:394
Async XLA Ops:
  0.0 15.1 %copy-start = (bf16[256,1024]{1,0:T(8,128)(2,1)S(1)}, bf16[256,1024]{1,0:T(8,128)(2,1)}, u32[]{:S(2)}) copy-start(bf16[256,1024]{1,0:T(8,128)(2,1)} %constant.2.clone.basis_ref) | copy-start | bytes 1572868

commit v3 on v2

--- a/solution.py
+++ b/solution.py
@@ -66,6 +66,7 @@
     share = sources // parts
     rows = tile // parts
     order = list(range(tiles - 1, -1, -1))
+    same_core_first = sorted(range(1, tiles), key=lambda r: (-(r // 2), r % 2))
     visits = chosen(visit_order(parts), me_z)
     small = tiles <= LIMIT
 
@@ -173,7 +174,7 @@
 
     def send_step(f, n):
         if small:
-            for r in order[:-1]:
+            for r in order[:-1] if n == 0 else same_core_first:
                 space_copy(f, n, r).start()
 
     def enter():

time: 17.6 us -> 17.4 us (0.989)
  Pallas kernels: 17.5 us -> 17.2 us
    pallas_call x1, Pallas kernels: 15.1 us -> 14.9 us  [shards(): pl.pallas_call(functools.partial(spectra_kernel, tiles, parts), out_shape...]
where the time goes in v3:
time: 17.4 us; the launch traced here: 17.3 us
  Pallas kernels  17.2 us (99%)
    pallas_call x1, Pallas kernels, shards(): pl.pallas_call(functools.partial(spectra_kernel, tiles, parts), out_shape...  14.9 us
    pallas_call x1, Pallas kernels, shards(): pl.pallas_call(functools.partial(time_kernel, share), out_shape=jax.Shape...  2.35 us

profile of v3, /device:TPU:0, one launch (start us, length us, event | category | flops | bytes accessed | tf_op | source)
XLA Modules:
  0.0 17.3 jit_solution(6380080531043597687)
XLA Ops:
  0.0 0.0 copy-start
  0.0 14.9 %spectra_kernel.1 = (bf16[4,2,128,128]{3,2,1,0:T(8,128)(2,1)S(1)}, bf16[4,2048,128]{2,1,0:T(8,128)(2,1)S(1)}) custom-call(s32[2,8,8]{2,1,0:T(8,128)} %ranks_hbm.1, bf16[2,2,256,128]{3,2,1,0:T(8,128)(2,1)} %recorded_hbm.1, bf16[2,8,512,128]{3,2,1,0:T(8,128)(2,1)} %bitcast.4, bf16[2,2,2048,128]{3,2,1,0:T(8,128)(2,1)} %bitcast.5, s32[32,256]{1,0:T(8,128)} %bitcast.6), custom_call_target="tpu_custom_call" | custom-call | tf_op jit(solution)/shard_map/spectra_kernel/pallas_call | solution.py:362
  14.9 0.0 copy-done
  14.9 2.4 %time_kernel.1 = f32[8192,128]{1,0:T(8,128)} custom-call(bf16[4,2,128,128]{3,2,1,0:T(8,128)(2,1)S(1)} %get-tuple-element.7.spec_ref, bf16[4,2048,128]{2,1,0:T(8,128)(2,1)S(1)} %get-tuple-element.8.mask_ref, bf16[256,1024]{1,0:T(8,128)(2,1)S(1)} %copy-done), custom_call_target="tpu_custom_call" | custom-call | tf_op jit(solution)/shard_map/time_kernel/pallas_call | solution.py:395
Async XLA Ops:
  0.0 14.9 %copy-start = (bf16[256,1024]{1,0:T(8,128)(2,1)S(1)}, bf16[256,1024]{1,0:T(8,128)(2,1)}, u32[]{:S(2)}) copy-start(bf16[256,1024]{1,0:T(8,128)(2,1)} %constant.2.clone.basis_ref) | copy-start | bytes 1572868

commit v4 on v3

--- a/solution.py
+++ b/solution.py
@@ -244,23 +244,28 @@
     swap_lane = lax.broadcasted_iota(jnp.int32, (rows, sources), 1)
     for n in range(parts):
         for f in range(freqs):
+            def product(blocks, splits):
+                plain, turned = [], []
+                for r in blocks:
+                    block = recv_ref[f, n, r]
+                    plain.append(block)
+                    swapped = pltpu.roll(block.astype(jnp.float32), half, 1)
+                    turned.append(jnp.where(low, -swapped, swapped).astype(jnp.bfloat16))
+                rhs = jnp.concatenate(
+                    [jnp.concatenate(plain, axis=1), jnp.concatenate(turned, axis=1)], axis=0
+                )
+                sides = []
+                for i in range(splits):
+                    span = pl.ds(i * tile // splits, tile // splits)
+                    lhs = jnp.concatenate(
+                        [factor_ref[f, span, r * ranks : (r + 1) * ranks] for r in blocks], axis=1
+                    )
+                    sides.append(lax.dot_general(lhs, rhs, NT_DIMS, preferred_element_type=jnp.float32))
+                return jnp.concatenate(sides, axis=0)
+
+            early = product((0, tiles), 2) if n == 0 and f == 0 else None
             arrivals(recv_ref.at[f, n], recv_sems.at[f, n]).wait()
-            plain, turned = [], []
-            for r in range(tiles + 1):
-                block = recv_ref[f, n, r]
-                plain.append(block)
-                swapped = pltpu.roll(block.astype(jnp.float32), half, 1)
-                turned.append(jnp.where(low, -swapped, swapped).astype(jnp.bfloat16))
-            rhs = jnp.concatenate(
-                [jnp.concatenate(plain, axis=1), jnp.concatenate(turned, axis=1)], axis=0
-            )
-            total = jnp.concatenate(
-                [
-                    lax.dot_general(factor_ref[f, at : at + tile // 2], rhs, NT_DIMS, preferred_element_type=jnp.float32)
-                    for at in (0, tile // 2)
-                ],
-                axis=0,
-            )
+            total = product(range(tiles + 1), 2) if early is None else product(range(1, tiles), 2) + early
             if total.shape[1] < sources:
                 total = jnp.concatenate([total, total], axis=1)
             for c in range(2):
@@ -302,9 +307,11 @@
 ):
     parts, freqs, rows, sources = spec_ref.shape
     rows //= 2
-    for n in range(rows // (2 * GROUP)):
+    chunks = [(0, (0,)), (0, (1,))] + [(n, (0, 1)) for n in range(1, rows // (2 * GROUP))]
+    for n, chosen_sides in chunks:
         sides = []
-        for g in (2 * n, 2 * n + 1):
+        for side in chosen_sides:
+            g = 2 * n + side
             pieces = []
             for z in range(parts):
                 for f in range(freqs):
@@ -319,19 +326,19 @@
             product = jnp.dot(
                 lhs, basis_ref[:, pair * 2 * NT : (pair + 1) * 2 * NT], preferred_element_type=jnp.float32
             )
-            for side in range(2):
+            for i, side in enumerate(chosen_sides):
                 for q in range(parts):
                     for e in range(2):
                         p = q * rows + (2 * n + side) * GROUP + pair * 2 + e
-                        at = side * sources + q * share
+                        at = i * sources + q * share
                         values = product[at : at + share, e * NT : (e + 1) * NT]
                         row = (q * 2 * GROUP + side * GROUP + pair * 2 + e) * share
                         mask = mask_ref[n, row : row + share].astype(jnp.float32)
                         rows_ref[p * share : (p + 1) * share, :] = values * mask
+        count = len(chosen_sides) * GROUP * share
         for q in range(parts):
-            span = pl.ds((q * rows + 2 * n * GROUP) * share, 2 * GROUP * share)
-            copy = pltpu.make_async_copy(rows_ref.at[span], out_hbm.at[span], out_sem)
-            copy.start()
+            span = pl.ds((q * rows + (2 * n + chosen_sides[0]) * GROUP) * share, count)
+            pltpu.make_async_copy(rows_ref.at[span], out_hbm.at[span], out_sem).start()
     pltpu.make_async_copy(rows_ref, out_hbm, out_sem).wait()
 
 

time: 17.4 us -> 17.3 us (level)
  no operation moved by 1% of the time
where the time goes in v4:
time: 17.3 us; the launch traced here: 17.2 us
  Pallas kernels  17.2 us (99%)
    pallas_call x1, Pallas kernels, shards(): pl.pallas_call(functools.partial(spectra_kernel, tiles, parts), out_shape...  14.9 us
    pallas_call x1, Pallas kernels, shards(): pl.pallas_call(functools.partial(time_kernel, share), out_shape=jax.Shape...  2.28 us

profile of v4, /device:TPU:0, one launch (start us, length us, event | category | flops | bytes accessed | tf_op | source)
XLA Modules:
  0.0 17.2 jit_solution(1390999112274035249)
XLA Ops:
  0.0 0.0 copy-start
  0.0 14.9 %spectra_kernel.1 = (bf16[4,2,128,128]{3,2,1,0:T(8,128)(2,1)S(1)}, bf16[4,2048,128]{2,1,0:T(8,128)(2,1)S(1)}) custom-call(s32[2,8,8]{2,1,0:T(8,128)} %ranks_hbm.1, bf16[2,2,256,128]{3,2,1,0:T(8,128)(2,1)} %recorded_hbm.1, bf16[2,8,512,128]{3,2,1,0:T(8,128)(2,1)} %bitcast.4, bf16[2,2,2048,128]{3,2,1,0:T(8,128)(2,1)} %bitcast.5, s32[32,256]{1,0:T(8,128)} %bitcast.6), custom_call_target="tpu_custom_call" | custom-call | tf_op jit(solution)/shard_map/spectra_kernel/pallas_call | solution.py:369
  14.9 0.0 copy-done
  14.9 2.3 %time_kernel.1 = f32[8192,128]{1,0:T(8,128)} custom-call(bf16[4,2,128,128]{3,2,1,0:T(8,128)(2,1)S(1)} %get-tuple-element.7.spec_ref, bf16[4,2048,128]{2,1,0:T(8,128)(2,1)S(1)} %get-tuple-element.8.mask_ref, bf16[256,1024]{1,0:T(8,128)(2,1)S(1)} %copy-done), custom_call_target="tpu_custom_call" | custom-call | tf_op jit(solution)/shard_map/time_kernel/pallas_call | solution.py:402
Async XLA Ops:
  0.0 14.9 %copy-start = (bf16[256,1024]{1,0:T(8,128)(2,1)S(1)}, bf16[256,1024]{1,0:T(8,128)(2,1)}, u32[]{:S(2)}) copy-start(bf16[256,1024]{1,0:T(8,128)(2,1)} %constant.2.clone.basis_ref) | copy-start | bytes 1572868
